TPU v7x, 512 devices: a whole 4x4x16 slice. The times are simulated.
512 devices in a mesh: wide: 64 (over y_lo, z, core), narrow: 8 (over y_hi, x).
Axes of the slice: x: 4, y: 4 (y_hi: 2, y_lo: 2; y = y_hi * 2 + y_lo), z: 16, core: 2. Of those that a mesh axis runs over, the one named last changes fastest.
Arguments:
- tokens: bfloat16 [8192, 2048], P('wide', 'narrow'), may hold values from -6 to 6
- expert_ids: int32 [8192, 6], P('wide'), may hold values from 0 to 63, all different within a row; in each aligned block of 128 rows (0 to 127, 128 to 255, ...) at most 14 rows name the same one
- route_weights: bfloat16 [8192, 6], P('wide'), may hold values from 0.049804688 to 0.5
- w_gate: bfloat16 [64, 1408, 2048], P('wide', 'narrow'), may hold values from -0.125 to 0.125
- w_up: bfloat16 [64, 1408, 2048], P('wide', 'narrow'), may hold values from -0.125 to 0.125
- w_down: bfloat16 [64, 1408, 2048], P('wide', 'narrow'), may hold values from -0.15625 to 0.15625
Outputs:
- mixed: bfloat16 [8192, 2048], P('wide', 'narrow')
Inputs may be any that keep to these rules, and one draw needn't show every extreme that they name: `expert_ids`: within a row the 6 experts differ. Among the 128 tokens of one aligned block, no expert is named more than 14 times, a bound that some block reaches.
All inputs are finite; a program needn't handle non-finite values.
Results may differ from a plain program's by a relative error of at most 0.017.
Values may be sent and summed in bfloat16 or wider, within the bound.
A program may use at most 64 MiB of HBM per device.

v0:
```python
import jax
import jax.numpy as jnp
from jax import lax
from jax.sharding import PartitionSpec as P


def local(tokens, expert_ids, route_weights, w_gate, w_up, w_down):
    tok_rows = expert_ids.shape[0]
    top_count = expert_ids.shape[1]
    local_experts = w_gate.shape[0]
    groups_wide = lax.axis_size("wide")
    experts_all = local_experts * groups_wide
    capacity = 7 * tok_rows * top_count // (6 * experts_all)
    slots_all = experts_all * capacity
    flat_ids = expert_ids.reshape(-1)
    onehot = (flat_ids[:, None] == jnp.arange(experts_all, dtype=jnp.int32)[None, :]).astype(
        jnp.int32
    )
    running = jnp.cumsum(onehot, axis=0)
    slot_index = jnp.sum(running * onehot, axis=1) - 1
    destination = (flat_ids * capacity + slot_index).reshape(tok_rows, top_count)
    hit = destination[:, :, None] == jnp.arange(slots_all, dtype=jnp.int32)[None, None, :]
    dispatch = jnp.any(hit, axis=1).astype(jnp.bfloat16)
    combine = jnp.sum(
        jnp.where(hit, route_weights.astype(jnp.float32)[:, :, None], 0.0), axis=1
    ).astype(jnp.bfloat16)
    outgoing = jnp.einsum("ts,td->sd", dispatch, tokens, preferred_element_type=jnp.float32).astype(
        jnp.bfloat16
    )
    received = lax.all_to_all(outgoing, "wide", split_axis=0, concat_axis=0, tiled=True)
    slot_rows = lax.all_gather(received, "narrow", axis=1, tiled=True)
    gate_proj = jnp.einsum("sd,fd->sf", slot_rows, w_gate[0], preferred_element_type=jnp.float32)
    up_proj = jnp.einsum("sd,fd->sf", slot_rows, w_up[0], preferred_element_type=jnp.float32)
    hidden = (jax.nn.silu(gate_proj) * up_proj).astype(jnp.bfloat16)
    partial_value = jnp.einsum(
        "sf,fd->sd", hidden, w_down[0], preferred_element_type=jnp.float32
    ).astype(jnp.bfloat16)
    summed = lax.psum_scatter(partial_value, "narrow", scatter_dimension=1, tiled=True)
    returned = lax.all_to_all(summed, "wide", split_axis=0, concat_axis=0, tiled=True)
    mixed = jnp.einsum("ts,sd->td", combine, returned, preferred_element_type=jnp.float32)
    return mixed.astype(jnp.bfloat16)


def solution(mesh):
    in_specs = (
        P("wide", "narrow"),
        P("wide", None),
        P("wide", None),
        P("wide", "narrow", None),
        P("wide", "narrow", None),
        P("wide", "narrow", None),
    )
    out_specs = P("wide", "narrow")
    return jax.shard_map(local, mesh=mesh, in_specs=in_specs, out_specs=out_specs, check_vma=False)
```

profile of v0, /device:TPU:1, one launch (start us, length us, event | category | flops | bytes accessed | tf_op | source)
XLA Modules:
  0.0 307.2 jit_solution(4234591035933541755)
XLA Ops:
  6.5 0.0 copy-start
  6.5 0.0 copy-start.2
  6.5 0.0 all-gather.2.cloned.1.call-start
  6.5 0.9 copy.21
  7.4 0.1 eq.42
  7.6 0.1 eq.38
  7.7 1.8 reduce-window.6
  9.5 0.3 slice_reduce_fusion
  9.8 0.1 fusion.15
  10.0 0.1 sub.7
  10.1 0.1 copy.24
  10.2 0.7 multiply_add_fusion
  10.9 0.4 fusion
  11.4 1.2 convolution_convert_fusion.1
  12.5 0.1 all_to_all.16
  12.7 49.6 %all_to_all.24 = bf16[64,14,256]{2,1,0:T(8,128)(2,1)S(1)} all-to-all(bf16[64,14,256]{2,1,0:T(8,128)(2,1)S(1)} %all_to_all.16), channel_id=1, replica_groups=mesh['wide'=64,'narrow'=8] {'wide'}, dimensions={0} | all-to-all | bytes 917504 | tf_op jit(solution)/shard_map/all_to_all | solution.py:30
  62.3 0.0 copy-start.3
  62.3 0.9 all_to_all.18
  63.2 0.0 all-gather.2.cloned.1.call-update
  63.3 0.0 reduce-scatter.2.cloned.1.call-start
  63.3 81.2 %all-gather.2.cloned.1.call-done = bf16[896,2048]{1,0:T(8,128)(2,1)} async-done(((bf16[896,256]{1,0:T(8,128)(2,1)}), bf16[896,2048]{1,0:T(8,128)(2,1)}) %all-gather.2.cloned.1.call-update) | async-done | bytes 3670032 | tf_op jit(solution)/shard_map/all_gather | solution.py:31
  144.5 0.0 copy-done.2
  144.5 3.4 %fusion.5 = f32[896,176]{0,1:T(8,128)S(1)} fusion(bf16[896,2048]{1,0:T(8,128)(2,1)} %all-gather.2.cloned.1.call-done, bf16[1,176,2048]{2,1,0:T(8,128)(2,1)S(1)} %copy-done.2), kind=kOutput, calls=%fused_computation.10 | convolution fusion | flops 645922816 | bytes 5021696 | tf_op jit(solution)/shard_map/sd,fd->sf/dot_general | solution.py:32
  147.9 0.0 copy-done
  147.9 0.0 copy-done.3
  147.9 6.5 %convolution_convert_fusion = bf16[896,2048]{1,0:T(8,128)(2,1)} fusion(bf16[896,2048]{1,0:T(8,128)(2,1)} %all-gather.2.cloned.1.call-done, bf16[1,176,2048]{2,1,0:T(8,128)(2,1)S(1)} %copy-done, bf16[1,176,2048]{2,1,0:T(8,128)(2,1)S(1)} %copy-done.3, f32[896,176]{0,1:T(8,128)S(1)} %fusion.5), kind=kOutput, calls=%fused_computation | convolution fusion | flops 1294626816 | bytes 9412608 | tf_op jit(solution)/shard_map/sf,fd->sd/dot_general | solution.py:35
  154.4 0.0 copy-start.1
  154.4 0.0 reduce-scatter.2.cloned.1.call-update
  154.4 96.4 %reduce-scatter.2.cloned.1.call-done = bf16[896,256]{1,0:T(8,128)(2,1)} async-done(((bf16[896,2048]{1,0:T(8,128)(2,1)}), bf16[896,256]{1,0:T(8,128)(2,1)}) %reduce-scatter.2.cloned.1.call-update) | async-done | bytes 458768 | tf_op jit(solution)/shard_map/reduce_scatter | solution.py:38
  250.8 1.9 all_to_all.19
  252.7 14.9 %all-to-all-start.1 = ((bf16[64,14,256]{2,1,0:T(8,128)(2,1)}), bf16[64,14,256]{2,1,0:T(8,128)(2,1)S(1)}, u32[]{:S(2)}, u32[]{:S(2)}) async-start(bf16[64,14,256]{2,1,0:T(8,128)(2,1)} %all_to_all.19), calls=%async_computation.2 | async-start | bytes 1048576 | tf_op jit(solution)/shard_map/all_to_all | solution.py:39
  267.7 0.0 copy-done.1
  267.7 0.3 select_reduce_fusion
  268.1 31.3 %all-to-all-done.1 = bf16[64,14,256]{2,1,0:T(8,128)(2,1)S(1)} async-done(((bf16[64,14,256]{2,1,0:T(8,128)(2,1)}), bf16[64,14,256]{2,1,0:T(8,128)(2,1)S(1)}, u32[]{:S(2)}, u32[]{:S(2)}) %all-to-all-start.1) | async-done | bytes 458784 | tf_op jit(solution)/shard_map/all_to_all | solution.py:39
  299.4 0.1 all_to_all.21
  299.5 0.9 convolution_convert_fusion.2
  (4 shorter events, 0.0 us)
Async XLA Ops:
  6.5 141.4 %copy-start = (bf16[1,176,2048]{2,1,0:T(8,128)(2,1)S(1)}, bf16[1,176,2048]{2,1,0:T(8,128)(2,1)}, u32[]{:S(2)}) copy-start(bf16[1,176,2048]{2,1,0:T(8,128)(2,1)} %param.11) | copy-start | bytes 2162692
  6.5 138.0 %copy-start.2 = (bf16[1,176,2048]{2,1,0:T(8,128)(2,1)S(1)}, bf16[1,176,2048]{2,1,0:T(8,128)(2,1)}, u32[]{:S(2)}) copy-start(bf16[1,176,2048]{2,1,0:T(8,128)(2,1)} %param.9) | copy-start | bytes 2162692
  6.5 138.0 %all-gather.2.cloned.1.call-start = ((), (), s32[]{:S(2)}) async-start(), calls=%async_computation.3 | async-start | bytes 4128768 | tf_op jit(solution)/shard_map/all_gather | solution.py:31
  62.3 85.6 %copy-start.3 = (bf16[1,176,2048]{2,1,0:T(8,128)(2,1)S(1)}, bf16[1,176,2048]{2,1,0:T(8,128)(2,1)}, u32[]{:S(2)}) copy-start(bf16[1,176,2048]{2,1,0:T(8,128)(2,1)} %param.10) | copy-start | bytes 2162692
  63.3 187.5 %reduce-scatter.2.cloned.1.call-start = ((), (), s32[]{:S(2)}) async-start(), calls=%async_computation.4 | async-start | bytes 4128768 | tf_op jit(solution)/shard_map/reduce_scatter | solution.py:38
  154.4 113.3 %copy-start.1 = (bf16[128,6]{0,1:T(8,128)(2,1)S(1)}, bf16[128,6]{0,1:T(8,128)(2,1)}, u32[]{:S(2)}) copy-start(bf16[128,6]{0,1:T(8,128)(2,1)} %param.8) | copy-start | bytes 4612
  252.7 46.6 %all-to-all-start.1 = ((bf16[64,14,256]{2,1,0:T(8,128)(2,1)}), bf16[64,14,256]{2,1,0:T(8,128)(2,1)S(1)}, u32[]{:S(2)}, u32[]{:S(2)}) async-start(bf16[64,14,256]{2,1,0:T(8,128)(2,1)} %all_to_all.19), calls=%async_computation.2 | async-start | bytes 1048576 | tf_op jit(solution)/shard_map/all_to_all | solution.py:39
Sparse Core Ops, SparseCore 0:
  63.4 81.0 all-gather.1
  154.5 96.2 reduce-scatter.1
where the time goes:
time: 308 us; the launch traced here: 307 us
  waiting for transfers between devices  209 us (68%)
  blocking collectives  49.6 us (16%)
  starting transfers between devices  15 us (5%)
  between operations  13.5 us (4%)
  matrix products  11.9 us (4%)
  local copies, waits for them, and re-layouts  4.76 us (2%)
  other arithmetic  3.48 us (1%)
    reduce_scatter x1, waiting for transfers between devices, local(): lax.psum_scatter(partial_value, 'narrow', scatter_dimension=1, tiled=True)  96.4 us
    all_gather x1, waiting for transfers between devices, local(): slot_rows = lax.all_gather(received, 'narrow', axis=1, tiled=True)  81.2 us
    all_to_all x1, blocking collectives, local(): lax.all_to_all(outgoing, 'wide', split_axis=0, concat_axis=0, tiled=True)  49.6 us
    all_to_all x1, waiting for transfers between devices, local(): lax.all_to_all(summed, 'wide', split_axis=0, concat_axis=0, tiled=True)  31.3 us
    all_to_all x1, starting transfers between devices, local(): lax.all_to_all(summed, 'wide', split_axis=0, concat_axis=0, tiled=True)  14.9 us
    dot_general x1, matrix products, local(): jnp.einsum('sf,fd->sd', hidden, w_down[0], preferred_element_type=jnp.flo...  6.47 us
  transfers between devices with their start and end apart: 3, of which 3 were waited for; matrix products, arithmetic and copies ran while one was open for 0% of the time, Pallas kernels for 0%

commit v1 on v0

--- a/solution.py
+++ b/solution.py
@@ -28,7 +28,10 @@
         jnp.bfloat16
     )
     received = lax.all_to_all(outgoing, "wide", split_axis=0, concat_axis=0, tiled=True)
-    slot_rows = lax.all_gather(received, "narrow", axis=1, tiled=True)
+    cover_lanes_over_axis = lambda local_x: jnp.concatenate(
+        lax.all_to_all(jnp.stack([local_x] * lax.axis_size("narrow"), 0), "narrow", 0, 0), 1
+    )
+    slot_rows = cover_lanes_over_axis(received)
     gate_proj = jnp.einsum("sd,fd->sf", slot_rows, w_gate[0], preferred_element_type=jnp.float32)
     up_proj = jnp.einsum("sd,fd->sf", slot_rows, w_up[0], preferred_element_type=jnp.float32)
     hidden = (jax.nn.silu(gate_proj) * up_proj).astype(jnp.bfloat16)

time: 308 us -> 267 us (0.87)
  waiting for transfers between devices: 209 us -> 118 us
  blocking collectives: 49.6 us -> 101 us
  matrix products: 11.9 us -> 8.78 us
    all_gather x1 -> x0, waiting for transfers between devices: 81.2 us -> none  [local(): slot_rows = lax.all_gather(received, 'narrow', axis=1, tiled=True)]
    all_to_all x0 -> x1, blocking collectives: none -> 51.2 us  [local(): lax.all_to_all(jnp.stack([local_x] * lax.axis_size('narrow'), 0), 'narrow...]
    reduce_scatter x1, waiting for transfers between devices: 96.4 us -> 86.9 us  [local(): lax.psum_scatter(partial_value, 'narrow', scatter_dimension=1, tiled=True)]
  transfers between devices with their start and end apart: 3 -> 2, of which waited for: 3 -> 2; matrix products, arithmetic and copies ran while one was open for 0% -> 0% of each run, Pallas kernels for 0% -> 0%
where the time goes in v1:
time: 267 us; the launch traced here: 266 us
  waiting for transfers between devices  118 us (44%)
  blocking collectives  101 us (38%)
  starting transfers between devices  14.9 us (6%)
  between operations  13.5 us (5%)
  matrix products  8.78 us (3%)
  local copies, waits for them, and re-layouts  6.5 us (2%)
  other arithmetic  3.48 us (1%)
    reduce_scatter x1, waiting for transfers between devices, local(): lax.psum_scatter(partial_value, 'narrow', scatter_dimension=1, tiled=True)  86.9 us
    all_to_all x1, blocking collectives, local(): lax.all_to_all(jnp.stack([local_x] * lax.axis_size('narrow'), 0), 'narrow...  51.2 us
    all_to_all x1, blocking collectives, local(): lax.all_to_all(outgoing, 'wide', split_axis=0, concat_axis=0, tiled=True)  49.6 us
    all_to_all x1, waiting for transfers between devices, local(): lax.all_to_all(summed, 'wide', split_axis=0, concat_axis=0, tiled=True)  31.3 us
    all_to_all x1, starting transfers between devices, local(): lax.all_to_all(summed, 'wide', split_axis=0, concat_axis=0, tiled=True)  14.9 us
    dot_general x1, matrix products, local(): jnp.einsum('sf,fd->sd', hidden, w_down[0], preferred_element_type=jnp.flo...  5.82 us
  transfers between devices with their start and end apart: 2, of which 2 were waited for; matrix products, arithmetic and copies ran while one was open for 0% of the time, Pallas kernels for 0%

profile of v1, /device:TPU:1, one launch (start us, length us, event | category | flops | bytes accessed | tf_op | source)
XLA Modules:
  0.0 266.4 jit_solution(10591090996789409102)
XLA Ops:
  6.5 0.0 copy-start
  6.5 0.0 reduce-scatter.2.cloned.1.call-start
  6.5 0.9 copy.23
  7.4 0.1 eq.42
  7.5 0.1 eq.38
  7.7 1.8 reduce-window.6
  9.5 0.3 slice_reduce_fusion
  9.8 0.1 fusion.15
  10.0 0.1 sub.7
  10.1 0.1 copy.26
  10.2 0.7 multiply_add_fusion
  10.9 0.4 fusion
  11.3 1.2 convolution_convert_fusion.1
  12.5 0.1 all_to_all.17
  12.6 49.6 %all_to_all.26 = bf16[64,14,256]{2,1,0:T(8,128)(2,1)S(1)} all-to-all(bf16[64,14,256]{2,1,0:T(8,128)(2,1)S(1)} %all_to_all.17), channel_id=1, replica_groups=mesh['wide'=64,'narrow'=8] {'wide'}, dimensions={0} | all-to-all | bytes 917504 | tf_op jit(solution)/shard_map/all_to_all | solution.py:30
  62.3 0.1 stack.4
  62.4 0.2 copy.27
  62.7 0.5 stack.5
  63.1 0.0 copy-start.2
  63.2 51.2 %all_to_all.27 = bf16[8,896,256]{1,2,0:T(8,128)(2,1)S(1)} all-to-all(bf16[8,896,256]{1,2,0:T(8,128)(2,1)S(1)} %stack.5), channel_id=1, replica_groups=mesh['wide'=64,'narrow'=8] {'narrow'}, dimensions={0} | all-to-all | bytes 7340032 | tf_op jit(solution)/shard_map/all_to_all | solution.py:32
  114.4 0.0 copy-start.1
  114.4 0.0 copy-start.4
  114.4 1.8 copy-done.1
  116.2 0.0 copy-done.2
  116.2 0.9 fusion.5
  117.2 0.0 copy-done
  117.2 0.0 copy-done.4
  117.2 5.8 %convolution_convert_fusion = bf16[896,2048]{1,0:T(8,128)(2,1)} fusion(bf16[896,2048]{0,1:T(8,128)(2,1)} %bitcast.36, bf16[1,176,2048]{2,1,0:T(8,128)(2,1)S(1)} %copy-done, bf16[1,176,2048]{2,1,0:T(8,128)(2,1)S(1)} %copy-done.4, f32[896,176]{0,1:T(8,128)S(1)} %fusion.5), kind=kOutput, calls=%fused_computation | convolution fusion | flops 1294626816 | bytes 9412608 | tf_op jit(solution)/shard_map/sf,fd->sd/dot_general | solution.py:38
  123.0 0.0 copy-start.3
  123.0 0.0 reduce-scatter.2.cloned.1.call-update
  123.0 86.9 %reduce-scatter.2.cloned.1.call-done = bf16[896,256]{1,0:T(8,128)(2,1)} async-done(((bf16[896,2048]{1,0:T(8,128)(2,1)}), bf16[896,256]{1,0:T(8,128)(2,1)}) %reduce-scatter.2.cloned.1.call-update) | async-done | bytes 458768 | tf_op jit(solution)/shard_map/reduce_scatter | solution.py:41
  209.9 1.9 all_to_all.20
  211.9 14.9 %all-to-all-start.2 = ((bf16[64,14,256]{2,1,0:T(8,128)(2,1)}), bf16[64,14,256]{2,1,0:T(8,128)(2,1)S(1)}, u32[]{:S(2)}, u32[]{:S(2)}) async-start(bf16[64,14,256]{2,1,0:T(8,128)(2,1)} %all_to_all.20), calls=%async_computation.3 | async-start | bytes 1048576 | tf_op jit(solution)/shard_map/all_to_all | solution.py:42
  226.8 0.0 copy-done.3
  226.9 0.3 select_reduce_fusion
  227.2 31.3 %all-to-all-done.2 = bf16[64,14,256]{2,1,0:T(8,128)(2,1)S(1)} async-done(((bf16[64,14,256]{2,1,0:T(8,128)(2,1)}), bf16[64,14,256]{2,1,0:T(8,128)(2,1)S(1)}, u32[]{:S(2)}, u32[]{:S(2)}) %all-to-all-start.2) | async-done | bytes 458784 | tf_op jit(solution)/shard_map/all_to_all | solution.py:42
  258.5 0.1 all_to_all.22
  258.7 0.9 convolution_convert_fusion.2
  (4 shorter events, 0.0 us)
Async XLA Ops:
  6.5 110.6 %copy-start = (bf16[1,176,2048]{2,1,0:T(8,128)(2,1)S(1)}, bf16[1,176,2048]{2,1,0:T(8,128)(2,1)}, u32[]{:S(2)}) copy-start(bf16[1,176,2048]{2,1,0:T(8,128)(2,1)} %param.11) | copy-start | bytes 2162692
  6.5 203.4 %reduce-scatter.2.cloned.1.call-start = ((), (), s32[]{:S(2)}) async-start(), calls=%async_computation.4 | async-start | bytes 4128768 | tf_op jit(solution)/shard_map/reduce_scatter | solution.py:41
  63.1 53.1 %copy-start.2 = (bf16[1,176,2048]{2,1,0:T(8,128)(2,1)S(1)}, bf16[1,176,2048]{2,1,0:T(8,128)(2,1)}, u32[]{:S(2)}) copy-start(bf16[1,176,2048]{2,1,0:T(8,128)(2,1)} %param.9) | copy-start | bytes 2162692
  114.4 1.8 copy-start.1
  114.4 2.8 %copy-start.4 = (bf16[1,176,2048]{2,1,0:T(8,128)(2,1)S(1)}, bf16[1,176,2048]{2,1,0:T(8,128)(2,1)}, u32[]{:S(2)}) copy-start(bf16[1,176,2048]{2,1,0:T(8,128)(2,1)} %param.10) | copy-start | bytes 2162692
  123.0 103.8 %copy-start.3 = (bf16[128,6]{0,1:T(8,128)(2,1)S(1)}, bf16[128,6]{0,1:T(8,128)(2,1)}, u32[]{:S(2)}) copy-start(bf16[128,6]{0,1:T(8,128)(2,1)} %param.8) | copy-start | bytes 4612
  211.9 46.6 %all-to-all-start.2 = ((bf16[64,14,256]{2,1,0:T(8,128)(2,1)}), bf16[64,14,256]{2,1,0:T(8,128)(2,1)S(1)}, u32[]{:S(2)}, u32[]{:S(2)}) async-start(bf16[64,14,256]{2,1,0:T(8,128)(2,1)} %all_to_all.20), calls=%async_computation.3 | async-start | bytes 1048576 | tf_op jit(solution)/shard_map/all_to_all | solution.py:42
Sparse Core Ops, SparseCore 0:
  123.2 86.7 reduce-scatter.1
